TPU v7x, 128 devices: a whole 4x4x4 slice. The times are simulated.
128 devices in a mesh: pipe: 8 (over x, z_hi), tensor: 16 (over z_lo, y, core).
Axes of the slice: x: 4, y: 4, z: 4 (z_hi: 2, z_lo: 2; z = z_hi * 2 + z_lo), core: 2. Of those that a mesh axis runs over, the one named last changes fastest.
Arguments:
- layer_input: bfloat16 [768, 8192], P('tensor', 'pipe'), may hold values from -6 to 6
- out_grad: bfloat16 [768, 8192], P('tensor', 'pipe'), may hold values from -2 to 2
- gate_pre: bfloat16 [768, 28672], P(None, 'tensor'), may hold values from -8 to 8
- up_pre: bfloat16 [768, 28672], P(None, 'tensor'), may hold values from -6 to 6
- gate_weight: bfloat16 [8192, 28672], P('pipe', 'tensor'), may hold values from -0.0625 to 0.0625
- up_weight: bfloat16 [8192, 28672], P('pipe', 'tensor'), may hold values from -0.0625 to 0.0625
- down_weight: bfloat16 [28672, 8192], P('tensor', 'pipe'), may hold values from -0.03125 to 0.03125
- gate_mask: int32 [64, 224], P('pipe', 'tensor'), may hold values from 0 to 1, as said below
- up_mask: int32 [64, 224], P('pipe', 'tensor'), may hold values from 0 to 1, as said below
- down_mask: int32 [224, 64], P('tensor', 'pipe'), may hold values from 0 to 1, as said below
Outputs:
- grad_input: bfloat16 [768, 8192], P('tensor', 'pipe')
- grad_gate: bfloat16 [8192, 28672], P('pipe', 'tensor')
- grad_up: bfloat16 [8192, 28672], P('pipe', 'tensor')
- grad_down: bfloat16 [28672, 8192], P('tensor', 'pipe')
Inputs may be any that keep to these rules, and one draw needn't show every extreme that they name: `gate_mask`: each entry is 1 for a kept block and 0 for a pruned one; the share of kept blocks differs from block column to block column. `up_mask`: each entry is 1 for a kept block and 0 for a pruned one; the share of kept blocks differs from block column to block column. `down_mask`: each entry is 1 for a kept block and 0 for a pruned one; the share of kept blocks differs from block row to block row.
All inputs are finite; a program needn't handle non-finite values.
Results may differ from a plain program's by a relative error of at most 0.005.
Values may be sent and summed in bfloat16 or wider, within the bound.
A program may use at most 128 MiB of HBM per device.

v0:
```python
import jax
import jax.numpy as jnp
from jax import lax
from jax.sharding import PartitionSpec as P

BLOCK = 128


def expand(mask):
    return jnp.repeat(jnp.repeat(mask, BLOCK, axis=0), BLOCK, axis=1)


def local_grads(hidden_grad, gate_val, up_val, sigma_val):
    gate_grad = (hidden_grad * up_val * sigma_val * (1.0 + gate_val * (1.0 - sigma_val))).astype(
        jnp.bfloat16
    )
    up_grad = (hidden_grad * gate_val * sigma_val).astype(jnp.bfloat16)
    return (gate_grad, up_grad)


def shards(
    layer_input,
    out_grad,
    gate_pre,
    up_pre,
    gate_weight,
    up_weight,
    down_weight,
    gate_mask,
    up_mask,
    down_mask,
):
    mask_gate = expand(gate_mask)
    mask_up = expand(up_mask)
    mask_down = expand(down_mask)
    gate_masked = gate_weight * mask_gate.astype(jnp.bfloat16)
    up_masked = up_weight * mask_up.astype(jnp.bfloat16)
    down_masked = down_weight * mask_down.astype(jnp.bfloat16)
    gate_val = gate_pre.astype(jnp.float32)
    up_val = up_pre.astype(jnp.float32)
    sigma_val = jax.nn.sigmoid(gate_val)
    hidden = (gate_val * sigma_val * up_val).astype(jnp.bfloat16)
    piece = lax.all_gather(out_grad, "tensor", axis=0, tiled=True)
    down_acc = lax.dot_general(
        hidden, piece, (((0,), (0,)), ((), ())), preferred_element_type=jnp.float32
    )
    partial_rows = lax.dot_general(
        piece, down_masked, (((1,), (1,)), ((), ())), preferred_element_type=jnp.float32
    )
    hidden_grad = partial_rows
    down_acc, hidden_partial = (down_acc, hidden_grad)
    grad_down = (down_acc * mask_down.astype(jnp.float32)).astype(jnp.bfloat16)
    hidden_grad = lax.psum(hidden_partial, "pipe")
    gate_grad, up_grad = local_grads(hidden_grad, gate_val, up_val, sigma_val)
    piece = lax.all_gather(layer_input, "tensor", axis=0, tiled=True)
    gate_rows = gate_grad
    up_rows = up_grad
    gate_acc = lax.dot_general(
        piece, gate_rows, (((0,), (0,)), ((), ())), preferred_element_type=jnp.float32
    )
    up_acc = lax.dot_general(
        piece, up_rows, (((0,), (0,)), ((), ())), preferred_element_type=jnp.float32
    )
    gate_acc, up_acc = (gate_acc, up_acc)
    grad_gate = (gate_acc * mask_gate.astype(jnp.float32)).astype(jnp.bfloat16)
    grad_up = (up_acc * mask_up.astype(jnp.float32)).astype(jnp.bfloat16)
    gate_rows = gate_grad
    up_rows = up_grad
    total = lax.dot_general(
        gate_rows, gate_masked, (((1,), (1,)), ((), ())), preferred_element_type=jnp.float32
    )
    grad_input = lax.psum_scatter(
        total
        + lax.dot_general(
            up_rows, up_masked, (((1,), (1,)), ((), ())), preferred_element_type=jnp.float32
        ),
        "tensor",
        scatter_dimension=0,
        tiled=True,
    ).astype(jnp.bfloat16)
    return (grad_input, grad_gate, grad_up, grad_down)


def solution(mesh):
    in_specs = (
        P("tensor", "pipe"),
        P("tensor", "pipe"),
        P(None, "tensor"),
        P(None, "tensor"),
        P("pipe", "tensor"),
        P("pipe", "tensor"),
        P("tensor", "pipe"),
        P("pipe", "tensor"),
        P("pipe", "tensor"),
        P("tensor", "pipe"),
    )
    out_specs = (P("tensor", "pipe"), P("pipe", "tensor"), P("pipe", "tensor"), P("tensor", "pipe"))
    return jax.shard_map(shards, mesh=mesh, in_specs=in_specs, out_specs=out_specs, check_vma=False)
```

profile of v0, /device:TPU:0, one launch (start us, length us, event | category | flops | bytes accessed | tf_op | source)
XLA Modules:
  0.0 404.0 jit_solution(1261620353858778361)
XLA Ops:
  7.2 0.7 all-gather.3.cloned.1.call-update
  7.9 0.8 fusion.17
  8.8 36.6 %all-gather.3.cloned.1.call-done = bf16[768,1024]{1,0:T(8,128)(2,1)} async-done(((bf16[48,1024]{1,0:T(8,128)(2,1)}), bf16[768,1024]{1,0:T(8,128)(2,1)}) %all-gather.3.cloned.1.call-update) | async-done | bytes 1572880 | tf_op jit(solution)/shard_map/all_gather | solution.py:43
  45.4 5.1 %broadcast_in_dim.31 = bf16[1792,8,128]{2,1,0:T(8,128)(2,1)S(1)} broadcast(bf16[1792,8]{1,0:T(8,128)(2,1)S(1)} %bitcast.66), dimensions={0,1} | broadcast | bytes 3698688 | tf_op jit(solution)/shard_map/broadcast_in_dim | solution.py:10
  50.6 6.4 %convolution_bitcast_fusion = f32[768,1792]{0,1:T(8,128)} fusion(bf16[768,1024]{1,0:T(8,128)(2,1)} %all-gather.3.cloned.1.call-done, bf16[1792,1024]{1,0:T(8,128)(2,1)S(1)} %copy-done.9, bf16[224,8,8,128]{3,2,1,0:T(8,128)(2,1)S(1)} %bitcast.64), kind=kOutput, calls=%fused_computation.22 | convolution fusion | flops 2820407296 | bytes 14417920 | tf_op jit(solution)/shard_map/dot_general | solution.py:47
  57.0 0.7 all-gather.5.cloned.1.call-update
  57.7 0.2 reduce-scatter.2.cloned.1.call-start
  58.0 3.3 copy.23
  61.3 4.5 %copy.24 = bf16[768,1792]{0,1:T(8,128)(2,1)} copy(bf16[768,1792]{1,0:T(8,128)(2,1)} %param.12) | data formatting | bytes 5505024 | tf_op args[2]
  65.8 0.1 copy.25
  65.9 0.1 broadcast_bitcast_fusion.3
  66.0 6.0 %copy.26 = bf16[1024,1792]{0,1:T(8,128)(2,1)} copy(bf16[1024,1792]{1,0:T(8,128)(2,1)} %param.14) | data formatting | bytes 7340032 | tf_op args[4]
  72.0 0.1 copy.27
  72.1 0.1 broadcast_bitcast_fusion.2
  72.3 6.0 %copy.28 = bf16[1024,1792]{0,1:T(8,128)(2,1)} copy(bf16[1024,1792]{1,0:T(8,128)(2,1)} %param.15) | data formatting | bytes 7340032 | tf_op args[5]
  78.2 4.3 %bitcast_multiply_fusion.6 = bf16[1024,1792]{0,1:T(8,128)(2,1)} fusion(bf16[1024,1792]{0,1:T(8,128)(2,1)} %copy.26, bf16[1024,14]{0,1:T(8,128)(2,1)S(1)} %bitcast.69), kind=kLoop, calls=%fused_computation.26 | loop fusion | flops 1835008 | bytes 7368704 | tf_op jit(solution)/shard_map/mul | solution.py:36
  82.5 2.1 bitcast_multiply_fusion.5
  84.6 207.2 %all-reduce.2.cloned.1.call-done = f32[768,1792]{0,1:T(8,128)} async-done(((f32[768,1792]{0,1:T(8,128)}), f32[768,1792]{0,1:T(8,128)}) %all-reduce.2.cloned.1.call-update) | async-done | bytes 5505040 | tf_op jit(solution)/shard_map/psum | solution.py:53
  291.8 5.0 %fusion.12 = (bf16[768,1792]{0,1:T(8,128)(2,1)S(1)}, bf16[768,1792]{0,1:T(8,128)(2,1)S(1)}) fusion(f32[768,1792]{0,1:T(8,128)} %all-reduce.2.cloned.1.call-done, bf16[768,1792]{0,1:T(8,128)(2,1)} %copy.24, bf16[768,1792]{0,1:T(8,128)(2,1)S(1)} %copy.23), kind=kLoop, calls=%fused_computation.21 | loop fusion | flops 20643840 | bytes 16515072 | tf_op jit(solution)/shard_map/convert_element_type | solution.py:17
  296.9 3.1 fusion.20
  300.0 0.9 copy-done.1
  300.9 4.9 %convolution_add_fusion = f32[768,1024]{1,0:T(8,128)} fusion(f32[768,1024]{1,0:T(8,128)S(1)} %fusion.20, bf16[768,1792]{0,1:T(8,128)(2,1)S(1)} %get-tuple-element.12, bf16[1024,1792]{0,1:T(8,128)(2,1)S(1)} %copy-done.1), kind=kOutput, calls=%fused_computation.28 | convolution fusion | flops 2819358720 | bytes 12713984 | tf_op jit(solution)/shard_map/dot_general | solution.py:74
  306.4 2.0 broadcast_in_dim.41
  308.5 0.2 copy-done.10
  308.7 5.2 %fusion = bf16[1792,1024]{1,0:T(8,128)(2,1)} fusion(f32[224,8,8,128]{3,2,1,0:T(8,128)S(1)} %bitcast.63, bf16[768,1024]{1,0:T(8,128)(2,1)S(1)} %copy-done.10, bf16[768,1792]{0,1:T(8,128)(2,1)S(1)} %copy.23, bf16[768,1792]{0,1:T(8,128)(2,1)S(1)} %copy-done.2), kind=kOutput, calls=%fused_computation.5 | convolution fusion | flops 2833252352 | bytes 18087936 | tf_op jit(solution)/shard_map/dot_general | solution.py:44
  313.9 14.5 %all-gather.5.cloned.1.call-done = bf16[768,1024]{1,0:T(8,128)(2,1)} async-done(((bf16[48,1024]{1,0:T(8,128)(2,1)}), bf16[768,1024]{1,0:T(8,128)(2,1)}) %all-gather.5.cloned.1.call-update) | async-done | bytes 1572880 | tf_op jit(solution)/shard_map/all_gather | solution.py:55
  328.4 7.1 %fusion.2 = bf16[1024,1792]{0,1:T(8,128)(2,1)} fusion(bf16[768,1792]{0,1:T(8,128)(2,1)} %copy-done.6, bf16[768,1024]{1,0:T(8,128)(2,1)} %all-gather.5.cloned.1.call-done, f32[1024,14]{0,1:T(8,128)S(1)} %bitcast.73), kind=kOutput, calls=%fused_computation.9 | convolution fusion | flops 2822242304 | bytes 8052736 | tf_op jit(solution)/shard_map/dot_general | solution.py:58
  335.5 6.1 %copy.32 = bf16[1024,1792]{1,0:T(8,128)(2,1)} copy(bf16[1024,1792]{0,1:T(8,128)(2,1)} %fusion.2) | data formatting | bytes 7340032
  341.6 6.2 %fusion.1 = bf16[1024,1792]{0,1:T(8,128)(2,1)} fusion(bf16[768,1792]{0,1:T(8,128)(2,1)S(1)} %copy-done.4, bf16[768,1024]{1,0:T(8,128)(2,1)} %all-gather.5.cloned.1.call-done, f32[1024,14]{0,1:T(8,128)S(1)} %bitcast.74), kind=kOutput, calls=%fused_computation.7 | convolution fusion | flops 2822242304 | bytes 8052736 | tf_op jit(solution)/shard_map/dot_general | solution.py:61
  347.8 5.9 %copy.33 = bf16[1024,1792]{1,0:T(8,128)(2,1)} copy(bf16[1024,1792]{0,1:T(8,128)(2,1)} %fusion.1) | data formatting | bytes 7340032
  353.7 42.1 %reduce-scatter.2.cloned.1.call-done = f32[48,1024]{1,0:T(8,128)} async-done(((f32[768,1024]{1,0:T(8,128)}), f32[48,1024]{1,0:T(8,128)}) %reduce-scatter.2.cloned.1.call-update) | async-done | bytes 196624 | tf_op jit(solution)/shard_map/reduce_scatter | solution.py:72
  395.9 1.6 convert_element_type.106
  (43 shorter events, 0.9 us)
Async XLA Ops:
  7.2 38.2 %all-gather.3.cloned.1.call-start = ((), (), s32[]{:S(2)}) async-start(), calls=%async_computation.1 | async-start | bytes 1671168 | tf_op jit(solution)/shard_map/all_gather | solution.py:43
  7.9 283.9 %all-reduce.2.cloned.1.call-start = ((), (), s32[]{:S(2)}) async-start(), calls=%async_computation.2 | async-start | bytes 11010048 | tf_op jit(solution)/shard_map/psum | solution.py:53
  45.4 5.2 %copy-start.9 = (bf16[1792,1024]{1,0:T(8,128)(2,1)S(1)}, bf16[1792,1024]{1,0:T(8,128)(2,1)}, u32[]{:S(2)}) copy-start(bf16[1792,1024]{1,0:T(8,128)(2,1)} %param.16) | copy-start | bytes 11010052
  57.0 271.4 %all-gather.5.cloned.1.call-start = ((), (), s32[]{:S(2)}) async-start(), calls=%async_computation.4 | async-start | bytes 1671168 | tf_op jit(solution)/shard_map/all_gather | solution.py:55
  57.7 338.2 %reduce-scatter.2.cloned.1.call-start = ((), (), s32[]{:S(2)}) async-start(), calls=%async_computation.3 | async-start | bytes 3342336 | tf_op jit(solution)/shard_map/reduce_scatter | solution.py:72
  61.3 4.5 %copy-start.7 = (s32[8,14]{1,0:T(8,128)S(1)}, s32[8,14]{1,0:T(8,128)}, u32[]{:S(2)}) copy-start(s32[8,14]{1,0:T(8,128)} %param.17) | copy-start | bytes 1348
  66.0 6.0 %copy-start.8 = (s32[8,14]{1,0:T(8,128)S(1)}, s32[8,14]{1,0:T(8,128)}, u32[]{:S(2)}) copy-start(s32[8,14]{1,0:T(8,128)} %param.18) | copy-start | bytes 1348
  78.2 4.3 %copy-start = (bf16[1024,1792]{0,1:T(8,128)(2,1)S(1)}, bf16[1024,1792]{0,1:T(8,128)(2,1)}, u32[]{:S(2)}) copy-start(bf16[1024,1792]{0,1:T(8,128)(2,1)} %copy.28) | copy-start | bytes 11010052
  291.8 5.1 %copy-start.5 = (bf16[1024,1792]{0,1:T(8,128)(2,1)S(1)}, bf16[1024,1792]{0,1:T(8,128)(2,1)}, u32[]{:S(2)}) copy-start(bf16[1024,1792]{0,1:T(8,128)(2,1)} %bitcast_multiply_fusion.6) | copy-start | bytes 11010052
  296.8 3.1 copy-start.6
  296.9 3.1 copy-start.3
  296.9 4.0 copy-start.1
  306.4 2.1 copy-start.2
  306.4 2.3 copy-start.10
  335.5 6.1 %copy-start.4 = (bf16[768,1792]{0,1:T(8,128)(2,1)S(1)}, bf16[768,1792]{0,1:T(8,128)(2,1)}, u32[]{:S(2)}) copy-start(bf16[768,1792]{0,1:T(8,128)(2,1)} %copy-done.3) | copy-start | bytes 8257540
Sparse Core Ops, SparseCore 0:
  9.7 35.6 all-gather.2
  57.1 234.6 all-reduce.1
  293.5 34.8 all-gather.4
  330.7 65.1 reduce-scatter.1
where the time goes:
time: 405 us; the launch traced here: 404 us
  waiting for transfers between devices  302 us (75%)
  local copies, waits for them, and re-layouts  41.1 us (10%)
  matrix products  32.9 us (8%)
  between operations  14 us (3%)
  other arithmetic  13.7 us (3%)
    psum x1, waiting for transfers between devices, shards(): hidden_grad = lax.psum(hidden_partial, 'pipe')  207 us
    reduce_scatter x1, waiting for transfers between devices, shards(): lax.psum_scatter(total + lax.dot_general(up_rows, up_masked, (((1,), (1,)...  42.1 us
    all_gather x1, waiting for transfers between devices, shards(): piece = lax.all_gather(out_grad, 'tensor', axis=0, tiled=True)  36.6 us
    unnamed x40, local copies, waits for them, and re-layouts  33.3 us
    all_gather x1, waiting for transfers between devices, shards(): piece = lax.all_gather(layer_input, 'tensor', axis=0, tiled=True)  14.5 us
  transfers between devices with their start and end apart: 4, of which 4 were waited for; matrix products, arithmetic and copies ran while one was open for 18% of the time, Pallas kernels for 0%

commit v1 on v0

--- a/solution.py
+++ b/solution.py
@@ -52,7 +52,9 @@
     grad_down = (down_acc * mask_down.astype(jnp.float32)).astype(jnp.bfloat16)
     hidden_grad = lax.psum(hidden_partial, "pipe")
     gate_grad, up_grad = local_grads(hidden_grad, gate_val, up_val, sigma_val)
-    piece = lax.all_gather(layer_input, "tensor", axis=0, tiled=True)
+    piece = jnp.concatenate(
+        lax.all_to_all(jnp.stack([layer_input] * lax.axis_size("tensor")), "tensor", 0, 0), axis=0
+    )
     gate_rows = gate_grad
     up_rows = up_grad
     gate_acc = lax.dot_general(

time: 405 us -> 392 us (0.968)
  waiting for transfers between devices: 302 us -> 281 us
  starting transfers between devices: 0.34 us -> 4.74 us
    reduce_scatter x1, waiting for transfers between devices: 42.1 us -> 18.4 us  [shards(): lax.psum_scatter(total + lax.dot_general(up_rows, up_masked, (((1,), (1,)...]
    all_to_all x0 -> x1, waiting for transfers between devices: none -> 17.1 us  [shards(): lax.all_to_all(jnp.stack([layer_input] * lax.axis_size('tensor')), 'tenso...]
    all_gather x1 -> x0, waiting for transfers between devices: 14.5 us -> none  [shards(): piece = lax.all_gather(layer_input, 'tensor', axis=0, tiled=True)]
    all_to_all x0 -> x1, starting transfers between devices: none -> 4.62 us  [shards(): lax.all_to_all(jnp.stack([layer_input] * lax.axis_size('tensor')), 'tenso...]
    unnamed x40 -> x42, local copies, waits for them, and re-layouts: 33.3 us -> 33.4 us
  transfers between devices with their start and end apart: 4 -> 4, of which waited for: 4 -> 4; matrix products, arithmetic and copies ran while one was open for 18% -> 16% of each run, Pallas kernels for 0% -> 0%
where the time goes in v1:
time: 392 us; the launch traced here: 389 us
  waiting for transfers between devices  281 us (72%)
  local copies, waits for them, and re-layouts  42.6 us (11%)
  matrix products  33 us (8%)
  between operations  14 us (4%)
  other arithmetic  13.7 us (3%)
  starting transfers between devices  4.74 us (1%)
    psum x1, waiting for transfers between devices, shards(): hidden_grad = lax.psum(hidden_partial, 'pipe')  208 us
    all_gather x1, waiting for transfers between devices, shards(): piece = lax.all_gather(out_grad, 'tensor', axis=0, tiled=True)  36.6 us
    unnamed x42, local copies, waits for them, and re-layouts  33.4 us
    reduce_scatter x1, waiting for transfers between devices, shards(): lax.psum_scatter(total + lax.dot_general(up_rows, up_masked, (((1,), (1,)...  18.4 us
    all_to_all x1, waiting for transfers between devices, shards(): lax.all_to_all(jnp.stack([layer_input] * lax.axis_size('tensor')), 'tenso...  17.1 us
  transfers between devices with their start and end apart: 4, of which 4 were waited for; matrix products, arithmetic and copies ran while one was open for 16% of the time, Pallas kernels for 0%

profile of v1, /device:TPU:0, one launch (start us, length us, event | category | flops | bytes accessed | tf_op | source)
XLA Modules:
  0.0 388.8 jit_solution(12885450111622329612)
XLA Ops:
  7.2 0.7 all-gather.2.cloned.1.call-update
  7.9 0.8 fusion.17
  8.8 36.6 %all-gather.2.cloned.1.call-done = bf16[768,1024]{1,0:T(8,128)(2,1)} async-done(((bf16[48,1024]{1,0:T(8,128)(2,1)}), bf16[768,1024]{1,0:T(8,128)(2,1)}) %all-gather.2.cloned.1.call-update) | async-done | bytes 1572880 | tf_op jit(solution)/shard_map/all_gather | solution.py:43
  45.4 5.1 %broadcast_in_dim.31 = bf16[1792,8,128]{2,1,0:T(8,128)(2,1)S(1)} broadcast(bf16[1792,8]{1,0:T(8,128)(2,1)S(1)} %bitcast.67), dimensions={0,1} | broadcast | bytes 3698688 | tf_op jit(solution)/shard_map/broadcast_in_dim | solution.py:10
  50.6 6.3 %convolution_bitcast_fusion = f32[768,1792]{0,1:T(8,128)} fusion(bf16[768,1024]{1,0:T(8,128)(2,1)} %all-gather.2.cloned.1.call-done, bf16[1792,1024]{1,0:T(8,128)(2,1)S(1)} %copy-done.10, bf16[224,8,8,128]{3,2,1,0:T(8,128)(2,1)S(1)} %bitcast.65), kind=kOutput, calls=%fused_computation.22 | convolution fusion | flops 2820407296 | bytes 14417920 | tf_op jit(solution)/shard_map/dot_general | solution.py:47
  57.0 3.3 copy.23
  60.3 4.5 %copy.24 = bf16[768,1792]{0,1:T(8,128)(2,1)} copy(bf16[768,1792]{1,0:T(8,128)(2,1)} %param.12) | data formatting | bytes 5505024 | tf_op args[2]
  64.8 0.1 copy.25
  64.9 0.1 broadcast_bitcast_fusion.3
  65.0 6.1 %copy.26 = bf16[1024,1792]{0,1:T(8,128)(2,1)} copy(bf16[1024,1792]{1,0:T(8,128)(2,1)} %param.14) | data formatting | bytes 7340032 | tf_op args[4]
  71.2 0.1 copy.27
  71.3 0.1 broadcast_bitcast_fusion.2
  71.4 5.9 %copy.28 = bf16[1024,1792]{0,1:T(8,128)(2,1)} copy(bf16[1024,1792]{1,0:T(8,128)(2,1)} %param.15) | data formatting | bytes 7340032 | tf_op args[5]
  77.4 4.3 %bitcast_multiply_fusion.6 = bf16[1024,1792]{0,1:T(8,128)(2,1)} fusion(bf16[1024,1792]{0,1:T(8,128)(2,1)} %copy.26, bf16[1024,14]{0,1:T(8,128)(2,1)S(1)} %bitcast.70), kind=kLoop, calls=%fused_computation.26 | loop fusion | flops 1835008 | bytes 7368704 | tf_op jit(solution)/shard_map/mul | solution.py:36
  81.6 2.1 bitcast_multiply_fusion.5
  83.7 208.0 %all-reduce.2.cloned.1.call-done = f32[768,1792]{0,1:T(8,128)} async-done(((f32[768,1792]{0,1:T(8,128)}), f32[768,1792]{0,1:T(8,128)}) %all-reduce.2.cloned.1.call-update) | async-done | bytes 5505040 | tf_op jit(solution)/shard_map/psum | solution.py:53
  291.7 5.0 %fusion.12 = (bf16[768,1792]{0,1:T(8,128)(2,1)S(1)}, bf16[768,1792]{0,1:T(8,128)(2,1)S(1)}) fusion(f32[768,1792]{0,1:T(8,128)} %all-reduce.2.cloned.1.call-done, bf16[768,1792]{0,1:T(8,128)(2,1)} %copy.24, bf16[768,1792]{0,1:T(8,128)(2,1)S(1)} %copy.23), kind=kLoop, calls=%fused_computation.21 | loop fusion | flops 20643840 | bytes 16515072 | tf_op jit(solution)/shard_map/convert_element_type | solution.py:17
  296.8 3.1 fusion.20
  299.9 0.9 copy-done.1
  300.8 4.9 %convolution_add_fusion = f32[768,1024]{1,0:T(8,128)} fusion(f32[768,1024]{1,0:T(8,128)S(1)} %fusion.20, bf16[768,1792]{0,1:T(8,128)(2,1)S(1)} %get-tuple-element.12, bf16[1024,1792]{0,1:T(8,128)(2,1)S(1)} %copy-done.1), kind=kOutput, calls=%fused_computation.28 | convolution fusion | flops 2819358720 | bytes 12713984 | tf_op jit(solution)/shard_map/dot_general | solution.py:76
  305.8 1.3 stack.2
  307.1 4.6 %all-to-all-start = ((bf16[16,48,1024]{2,1,0:T(8,128)(2,1)}), bf16[16,48,1024]{2,1,0:T(8,128)(2,1)}, u32[]{:S(2)}, u32[]{:S(2)}) async-start(bf16[16,48,1024]{2,1,0:T(8,128)(2,1)} %stack.2), calls=%async_computation.1 | async-start | bytes 3145728 | tf_op jit(solution)/shard_map/all_to_all | solution.py:56
  312.3 2.0 broadcast_in_dim.41
  314.4 0.2 copy-done.11
  314.5 5.2 %fusion = bf16[1792,1024]{1,0:T(8,128)(2,1)} fusion(f32[224,8,8,128]{3,2,1,0:T(8,128)S(1)} %bitcast.64, bf16[768,1024]{1,0:T(8,128)(2,1)S(1)} %copy-done.11, bf16[768,1792]{0,1:T(8,128)(2,1)S(1)} %copy.23, bf16[768,1792]{0,1:T(8,128)(2,1)S(1)} %copy-done.2), kind=kOutput, calls=%fused_computation.5 | convolution fusion | flops 2833252352 | bytes 18087936 | tf_op jit(solution)/shard_map/dot_general | solution.py:44
  319.7 17.1 %all-to-all-done = bf16[16,48,1024]{2,1,0:T(8,128)(2,1)} async-done(((bf16[16,48,1024]{2,1,0:T(8,128)(2,1)}), bf16[16,48,1024]{2,1,0:T(8,128)(2,1)}, u32[]{:S(2)}, u32[]{:S(2)}) %all-to-all-start) | async-done | bytes 1572896 | tf_op jit(solution)/shard_map/all_to_all | solution.py:56
  336.8 7.1 %fusion.2 = bf16[1024,1792]{0,1:T(8,128)(2,1)} fusion(bf16[768,1792]{0,1:T(8,128)(2,1)} %copy-done.6, bf16[768,1024]{1,0:T(8,128)(2,1)} %bitcast.4, f32[1024,14]{0,1:T(8,128)S(1)} %bitcast.74), kind=kOutput, calls=%fused_computation.9 | convolution fusion | flops 2822242304 | bytes 8052736 | tf_op jit(solution)/shard_map/dot_general | solution.py:60
  344.0 6.1 %copy.32 = bf16[1024,1792]{1,0:T(8,128)(2,1)} copy(bf16[1024,1792]{0,1:T(8,128)(2,1)} %fusion.2) | data formatting | bytes 7340032
  350.1 6.3 %fusion.1 = bf16[1024,1792]{0,1:T(8,128)(2,1)} fusion(bf16[768,1792]{0,1:T(8,128)(2,1)S(1)} %copy-done.4, bf16[768,1024]{1,0:T(8,128)(2,1)} %bitcast.4, f32[1024,14]{0,1:T(8,128)S(1)} %bitcast.75), kind=kOutput, calls=%fused_computation.7 | convolution fusion | flops 2822242304 | bytes 8052736 | tf_op jit(solution)/shard_map/dot_general | solution.py:63
  356.4 5.9 %copy.33 = bf16[1024,1792]{1,0:T(8,128)(2,1)} copy(bf16[1024,1792]{0,1:T(8,128)(2,1)} %fusion.1) | data formatting | bytes 7340032
  362.3 18.4 %reduce-scatter.2.cloned.1.call-done = f32[48,1024]{1,0:T(8,128)} async-done(((f32[768,1024]{1,0:T(8,128)}), f32[48,1024]{1,0:T(8,128)}) %reduce-scatter.2.cloned.1.call-update) | async-done | bytes 196624 | tf_op jit(solution)/shard_map/reduce_scatter | solution.py:74
  380.6 1.6 convert_element_type.106
  (45 shorter events, 0.9 us)
Async XLA Ops:
  7.2 38.2 %all-gather.2.cloned.1.call-start = ((), (), s32[]{:S(2)}) async-start(), calls=%async_computation.2 | async-start | bytes 1671168 | tf_op jit(solution)/shard_map/all_gather | solution.py:43
  7.9 283.8 %all-reduce.2.cloned.1.call-start = ((), (), s32[]{:S(2)}) async-start(), calls=%async_computation.3 | async-start | bytes 11010048 | tf_op jit(solution)/shard_map/psum | solution.py:53
  45.4 5.2 %copy-start.10 = (bf16[1792,1024]{1,0:T(8,128)(2,1)S(1)}, bf16[1792,1024]{1,0:T(8,128)(2,1)}, u32[]{:S(2)}) copy-start(bf16[1792,1024]{1,0:T(8,128)(2,1)} %param.16) | copy-start | bytes 11010052
  56.9 323.7 %reduce-scatter.2.cloned.1.call-start = ((), (), s32[]{:S(2)}) async-start(), calls=%async_computation.4 | async-start | bytes 3342336 | tf_op jit(solution)/shard_map/reduce_scatter | solution.py:74
  60.3 4.5 %copy-start.8 = (s32[8,14]{1,0:T(8,128)S(1)}, s32[8,14]{1,0:T(8,128)}, u32[]{:S(2)}) copy-start(s32[8,14]{1,0:T(8,128)} %param.17) | copy-start | bytes 1348
  65.0 6.2 %copy-start.9 = (s32[8,14]{1,0:T(8,128)S(1)}, s32[8,14]{1,0:T(8,128)}, u32[]{:S(2)}) copy-start(s32[8,14]{1,0:T(8,128)} %param.18) | copy-start | bytes 1348
  77.4 4.3 %copy-start = (bf16[1024,1792]{0,1:T(8,128)(2,1)S(1)}, bf16[1024,1792]{0,1:T(8,128)(2,1)}, u32[]{:S(2)}) copy-start(bf16[1024,1792]{0,1:T(8,128)(2,1)} %copy.28) | copy-start | bytes 11010052
  291.7 5.1 %copy-start.5 = (bf16[1024,1792]{0,1:T(8,128)(2,1)S(1)}, bf16[1024,1792]{0,1:T(8,128)(2,1)}, u32[]{:S(2)}) copy-start(bf16[1024,1792]{0,1:T(8,128)(2,1)} %bitcast_multiply_fusion.6) | copy-start | bytes 11010052
  296.8 3.1 copy-start.6
  296.8 3.1 copy-start.3
  296.8 4.0 %copy-start.1 = (bf16[1024,1792]{0,1:T(8,128)(2,1)S(1)}, bf16[1024,1792]{0,1:T(8,128)(2,1)}, u32[]{:S(2)}) copy-start(bf16[1024,1792]{0,1:T(8,128)(2,1)} %bitcast_multiply_fusion.5) | copy-start | bytes 11010052
  300.8 5.0 %copy-start.7 = (bf16[48,1024]{1,0:T(8,128)(2,1)S(1)}, bf16[48,1024]{1,0:T(8,128)(2,1)}, u32[]{:S(2)}) copy-start(bf16[48,1024]{1,0:T(8,128)(2,1)} %param.10) | copy-start | bytes 294916
  307.1 29.7 %all-to-all-start = ((bf16[16,48,1024]{2,1,0:T(8,128)(2,1)}), bf16[16,48,1024]{2,1,0:T(8,128)(2,1)}, u32[]{:S(2)}, u32[]{:S(2)}) async-start(bf16[16,48,1024]{2,1,0:T(8,128)(2,1)} %stack.2), calls=%async_computation.1 | async-start | bytes 3145728 | tf_op jit(solution)/shard_map/all_to_all | solution.py:56
  312.3 2.1 copy-start.2
  312.3 2.2 copy-start.11
  344.0 6.1 %copy-start.4 = (bf16[768,1792]{0,1:T(8,128)(2,1)S(1)}, bf16[768,1792]{0,1:T(8,128)(2,1)}, u32[]{:S(2)}) copy-start(bf16[768,1792]{0,1:T(8,128)(2,1)} %copy-done.3) | copy-start | bytes 8257540
Sparse Core Ops, SparseCore 0:
  9.7 35.6 all-gather.1
  57.0 234.6 all-reduce.1
  305.9 74.7 reduce-scatter.1
